TPU v7x, 32 devices: a whole 2x2x4 slice. The times are simulated.
32 devices in a mesh: segment: 4 (over x, core), strip: 8 (over z, y).
Axes of the slice: x: 2, y: 2, z: 4, core: 2. Of those that a mesh axis runs over, the one named last changes fastest.
Arguments:
- held_blocks: bfloat16 [4, 4, 64, 12, 384], P('segment', None, 'strip'), may hold values from -6 to 6
- incoming: bfloat16 [1, 4, 64, 12, 384], P(None, None, 'strip'), may hold values from -6 to 6
- frame_counts: int32 [5], replicated, may hold values from 1 to 4, as said below
- first_cache: bfloat16 [4, 2, 64, 12, 384], P('segment', None, 'strip'), may hold values from -0.25 to 2
- second_cache: bfloat16 [4, 2, 64, 12, 384], P('segment', None, 'strip'), may hold values from -0.25 to 2
- first_kernel: bfloat16 [4, 3, 3, 3, 384, 384], P('segment'), may hold values from -0.0625 to 0.0625
- first_bias: float32 [4, 384], P('segment'), may hold values from -3 to 3
- first_gain: float32 [4, 384], P('segment'), may hold values from 0.5 to 2
- second_kernel: bfloat16 [4, 3, 3, 3, 384, 384], P('segment'), may hold values from -0.0625 to 0.0625
- second_bias: float32 [4, 384], P('segment'), may hold values from -3 to 3
- second_gain: float32 [4, 384], P('segment'), may hold values from 0.5 to 2
Outputs:
- section_out: bfloat16 [2, 4, 4, 64, 12, 384], P(None, 'segment', None, 'strip')
- first_cache_out: bfloat16 [4, 2, 64, 12, 384], P('segment', None, 'strip')
- second_cache_out: bfloat16 [4, 2, 64, 12, 384], P('segment', None, 'strip')
Inputs may be any that keep to these rules, and one draw needn't show every extreme that they name: `frame_counts`: the section at segment index s works at tick t (from 0) on block 3 - s + t; both 1 and 4 occur in every draw.
All inputs are finite; a program needn't handle non-finite values.
Results may differ from a plain program's by a relative error of at most 0.0051.
Values may be sent and summed in bfloat16 or wider, within the bound.
A program may use at most 128 MiB of HBM per device.

v0:
```python
import jax
import jax.numpy as jnp
from jax import lax
from jax.experimental import pallas as pl
from jax.experimental.pallas import tpu as pltpu
from jax.sharding import PartitionSpec as P

EPSILON = 1e-06
MESH = pl.DeviceIdType.MESH
WIDE = 16


def normed(values, channel_gain):
    factor = lax.rsqrt(jnp.mean(values * values, axis=-1, keepdims=True) + EPSILON)
    scaled = values * factor * channel_gain
    return scaled / (1.0 + jnp.exp(-scaled))


def kernel(
    counts, held, incoming, first_cache, second_cache, first_kernel, first_bias, first_gain,
    second_kernel, second_bias, second_gain, out, first_out, second_out,
    raw, fcache, scache, w1, w2, x1, x2, acc, local_sem, w_sem, send_sem, recv_sem,
):
    ticks, frames, height, cols = out.shape[0], out.shape[2], out.shape[3], out.shape[4]
    channels = out.shape[5]
    sections, strips = lax.axis_size("segment"), lax.axis_size("strip")
    s, p = lax.axis_index("segment"), lax.axis_index("strip")
    is_top, is_bottom = p == 0, p == strips - 1

    local = [
        pltpu.make_async_copy(held.at[0], raw.at[0, :, 2 : height + 2], local_sem.at[0]),
        pltpu.make_async_copy(first_cache.at[0], fcache.at[:, 2 : height + 2], local_sem.at[1]),
        pltpu.make_async_copy(second_cache.at[0], scache.at[:, 1 : height + 1], local_sem.at[2]),
    ]
    for copy in local:
        copy.start()
    fresh = pltpu.make_async_copy(incoming.at[0], raw.at[1, :, 2 : height + 2], local_sem.at[3])

    def weight(source, target, which, a, b, c):
        return pltpu.make_async_copy(
            source.at[0, a, b, c],
            target.at[a, pl.ds(b * channels, channels), pl.ds(c * channels, channels)],
            w_sem.at[which, a],
        )

    around = [(i, j) for i in (-1, 0, 1) for j in (-1, 0, 1) if (i, j) != (0, 0)]
    barrier = pltpu.get_barrier_semaphore()

    def exists(i, j):
        return (s + i >= 0) & (s + i < sections) & (p + j >= 0) & (p + j < strips)

    for i, j in around:
        @pl.when(exists(i, j))
        def _(i=i, j=j):
            pl.semaphore_signal(barrier, inc=1, device_id=(s + i, p + j), device_id_type=MESH)

    for a in range(3):
        for b in range(3):
            for c in range(3):
                weight(first_kernel, w1, 0, a, b, c).start()

    pl.semaphore_wait(barrier, sum(exists(i, j).astype(jnp.int32) for i, j in around))

    def remote(source, target, k, i, j):
        return pltpu.make_async_remote_copy(
            src_ref=source, dst_ref=target, send_sem=send_sem.at[k], recv_sem=recv_sem.at[k],
            device_id=(s + i, p + j), device_id_type=MESH,
        )

    def to_next(block, slot, k, i):
        return remote(block.at[:, height - 2 : height], raw.at[slot, :, 0:2], k, i, 1)

    def to_previous(block, slot, k, i):
        return remote(block.at[:, 0:2], raw.at[slot, :, height + 2 : height + 4], k, i, -1)

    def next_edges():
        return [
            to_next(held.at[0], 0, 0, 0),
            remote(first_cache.at[0, :, height - 2 : height], fcache.at[:, 0:2], 1, 0, 1),
            remote(second_cache.at[0, :, height - 1 : height], scache.at[:, 0:1], 2, 0, 1),
        ]

    def previous_edges():
        return [
            to_previous(held.at[0], 0, 3, 0),
            remote(first_cache.at[0, :, 0:2], fcache.at[:, height + 2 : height + 4], 4, 0, -1),
            remote(second_cache.at[0, :, 0:1], scache.at[:, height + 1 : height + 2], 5, 0, -1),
        ]

    @pl.when(jnp.logical_not(is_bottom))
    def _():
        for copy in next_edges():
            copy.start()

    @pl.when(jnp.logical_not(is_top))
    def _():
        for copy in previous_edges():
            copy.start()

    @pl.when(s == 0)
    def _():
        fresh.start()

        @pl.when(jnp.logical_not(is_bottom))
        def _():
            to_next(incoming.at[0], 1, 6, 0).start()

        @pl.when(jnp.logical_not(is_top))
        def _():
            to_previous(incoming.at[0], 1, 7, 0).start()

    for a in range(3):
        for b in range(3):
            for c in range(3):
                weight(second_kernel, w2, 1, a, b, c).start()

    x1[...] = jnp.zeros_like(x1)
    x2[...] = jnp.zeros_like(x2)

    @pl.when(is_top)
    def _():
        raw[:, :, 0:2] = jnp.zeros((ticks, frames, 2, cols, channels), raw.dtype)
        fcache[:, 0:2] = jnp.zeros((2, 2, cols, channels), raw.dtype)
        scache[:, 0:1] = jnp.zeros((2, 1, cols, channels), raw.dtype)

    @pl.when(is_bottom)
    def _():
        raw[:, :, height + 2 :] = jnp.zeros((ticks, frames, 2, cols, channels), raw.dtype)
        fcache[:, height + 2 :] = jnp.zeros((2, 2, cols, channels), raw.dtype)
        scache[:, height + 1 :] = jnp.zeros((2, 1, cols, channels), raw.dtype)

    for copy in local:
        copy.wait()

    @pl.when(jnp.logical_not(is_top))
    def _():
        for copy in next_edges():
            copy.wait_recv()

    @pl.when(jnp.logical_not(is_bottom))
    def _():
        for copy in previous_edges():
            copy.wait_recv()

    x1[0:2, :, 0:cols] = fcache[...]
    x2[0:2, :, 0:cols] = scache[...]

    def convolve(window, weights, source, which, rows, tick):
        span = rows * WIDE

        @pl.loop(0, 3)
        def _(a):
            @pl.when(tick == 0)
            def _():
                for b in range(3):
                    for c in range(3):
                        weight(source, weights, which, a, b, c).wait()

            lhs = jnp.concatenate(
                [
                    window[pl.ds(a, frames), b : b + rows].reshape(frames * span, channels)
                    for b in range(3)
                ],
                axis=-1,
            )
            product = jnp.dot(lhs, weights[a], preferred_element_type=jnp.float32)

            @pl.when(a == 0)
            def _():
                acc[0 : frames * span] = product

            @pl.when(a > 0)
            def _():
                acc[0 : frames * span] += product

    def summed(f, rows, bias):
        span = rows * WIDE
        at = pl.ds(pl.multiple_of(f * span, span), span)
        left = pltpu.roll(acc[at, 0:channels], 1, 0)
        right = pltpu.roll(acc[at, 2 * channels : 3 * channels], span - 1, 0)
        total = left + acc[at, channels : 2 * channels] + right + bias
        return total.reshape(rows, WIDE, channels)

    @pl.loop(0, ticks)
    def _(tick):
        live = counts[sections - 1 - s + tick]

        @pl.when(tick > 0)
        def _():
            @pl.when(s == 0)
            def _():
                fresh.wait()

                @pl.when(jnp.logical_not(is_top))
                def _():
                    to_next(incoming.at[0], 1, 6, 0).wait_recv()

                @pl.when(jnp.logical_not(is_bottom))
                def _():
                    to_previous(incoming.at[0], 1, 7, 0).wait_recv()

            @pl.when(s > 0)
            def _():
                remote(out.at[0, 0], raw.at[1, :, 2 : height + 2], 8, 1, 0).wait_recv()

                @pl.when(jnp.logical_not(is_top))
                def _():
                    to_next(out.at[0, 0], 1, 9, 1).wait_recv()

                @pl.when(jnp.logical_not(is_bottom))
                def _():
                    to_previous(out.at[0, 0], 1, 10, 1).wait_recv()

        @pl.loop(0, frames)
        def _(f):
            values = jnp.where(f < live, raw[tick, f].astype(jnp.float32), 0.0)
            x1[2 + f, :, 0:cols] = normed(values, first_gain[...]).astype(jnp.bfloat16)

        convolve(x1, w1, first_kernel, 0, height + 2, tick)

        @pl.loop(0, frames)
        def _(f):
            shape = (height + 2, WIDE, 1)
            row = lax.broadcasted_iota(jnp.int32, shape, 0)
            col = lax.broadcasted_iota(jnp.int32, shape, 1)
            low = jnp.where(is_top, 1, 0)
            high = jnp.where(is_bottom, height, height + 1)
            high = jnp.where(f < live, high, -1)
            keep = (row >= low) & (row <= high) & (col < cols)
            hidden = jnp.where(keep, summed(f, height + 2, first_bias[...]), 0.0)
            x2[2 + f] = normed(hidden, second_gain[...]).astype(jnp.bfloat16)

        convolve(x2, w2, second_kernel, 1, height, tick)

        @pl.loop(0, frames)
        def _(f):
            total = summed(f, height, second_bias[...])[:, 0:cols]
            total = total + raw[tick, f, 2 : height + 2].astype(jnp.float32)
            out[tick, 0, f] = jnp.where(f < live, total, 0.0).astype(jnp.bfloat16)

        @pl.when((tick == 0) & (s < sections - 1))
        def _():
            remote(out.at[0, 0], raw.at[1, :, 2 : height + 2], 8, 1, 0).start()

            @pl.when(jnp.logical_not(is_bottom))
            def _():
                to_next(out.at[0, 0], 1, 9, 1).start()

            @pl.when(jnp.logical_not(is_top))
            def _():
                to_previous(out.at[0, 0], 1, 10, 1).start()

        for window in (x1, x2):
            for j in range(2):
                window[j] = window[live + j]

    first_out[0] = x1[0:2, 2 : height + 2, 0:cols]
    second_out[0] = x2[0:2, 1 : height + 1, 0:cols]

    @pl.when(jnp.logical_not(is_bottom))
    def _():
        for copy in next_edges():
            copy.wait_send()

        @pl.when(s == 0)
        def _():
            to_next(incoming.at[0], 1, 6, 0).wait_send()

        @pl.when(s < sections - 1)
        def _():
            to_next(out.at[0, 0], 1, 9, 1).wait_send()

    @pl.when(jnp.logical_not(is_top))
    def _():
        for copy in previous_edges():
            copy.wait_send()

        @pl.when(s == 0)
        def _():
            to_previous(incoming.at[0], 1, 7, 0).wait_send()

        @pl.when(s < sections - 1)
        def _():
            to_previous(out.at[0, 0], 1, 10, 1).wait_send()

    @pl.when(s < sections - 1)
    def _():
        remote(out.at[0, 0], raw.at[1, :, 2 : height + 2], 8, 1, 0).wait_send()


def on_device(
    held_blocks, incoming, frame_counts, first_cache, second_cache, first_kernel, first_bias,
    first_gain, second_kernel, second_bias, second_gain,
):
    _, frames, height, cols, channels = held_blocks.shape
    ticks = incoming.shape[0] + 1
    bf16 = jnp.bfloat16
    anywhere = pl.BlockSpec(memory_space=pltpu.HBM)
    inside = pl.BlockSpec(memory_space=pltpu.VMEM)
    return pl.pallas_call(
        kernel,
        out_shape=(
            jax.ShapeDtypeStruct((ticks, 1, frames, height, cols, channels), bf16),
            jax.ShapeDtypeStruct(first_cache.shape, bf16),
            jax.ShapeDtypeStruct(second_cache.shape, bf16),
        ),
        in_specs=[pl.BlockSpec(memory_space=pltpu.SMEM)] + [anywhere] * 5
        + [inside, inside, anywhere, inside, inside],
        out_specs=(inside, inside, inside),
        scratch_shapes=[
            pltpu.VMEM((ticks, frames, height + 4, cols, channels), bf16),
            pltpu.VMEM((2, height + 4, cols, channels), bf16),
            pltpu.VMEM((2, height + 2, cols, channels), bf16),
            pltpu.VMEM((3, 3 * channels, 3 * channels), bf16),
            pltpu.VMEM((3, 3 * channels, 3 * channels), bf16),
            pltpu.VMEM((frames + 2, height + 4, WIDE, channels), bf16),
            pltpu.VMEM((frames + 2, height + 2, WIDE, channels), bf16),
            pltpu.VMEM((frames * (height + 2) * WIDE, 3 * channels), jnp.float32),
            pltpu.SemaphoreType.DMA((4,)),
            pltpu.SemaphoreType.DMA((2, 3)),
            pltpu.SemaphoreType.DMA((11,)),
            pltpu.SemaphoreType.DMA((11,)),
        ],
        compiler_params=pltpu.CompilerParams(
            collective_id=0, has_side_effects=True, vmem_limit_bytes=60 * 1024 * 1024
        ),
    )(
        frame_counts, held_blocks, incoming, first_cache, second_cache, first_kernel, first_bias,
        first_gain, second_kernel, second_bias, second_gain,
    )


def solution(mesh):
    return jax.shard_map(
        on_device,
        mesh=mesh,
        in_specs=(
            P("segment", None, "strip", None, None),
            P(None, None, "strip", None, None),
            P(),
            P("segment", None, "strip", None, None),
            P("segment", None, "strip", None, None),
            P("segment", None, None, None, None, None),
            P("segment", None),
            P("segment", None),
            P("segment", None, None, None, None, None),
            P("segment", None),
            P("segment", None),
        ),
        out_specs=(
            P(None, "segment", None, "strip", None, None),
            P("segment", None, "strip", None, None),
            P("segment", None, "strip", None, None),
        ),
        check_vma=False,
    )
```

profile of v0, /device:TPU:18, one launch (start us, length us, event | category | flops | bytes accessed | tf_op | source)
XLA Modules:
  0.0 67.4 jit_solution(8976337026476874809)
XLA Ops:
  0.6 1.6 %copy.16.first_cache = bf16[1,2,8,12,384]{4,3,2,1,0:T(8,128)(2,1)} copy(bf16[1,2,8,12,384]{4,2,3,1,0:T(8,128)(2,1)} %param.14) | data formatting | bytes 294912 | tf_op args[3]
  2.2 1.6 %copy.17.second_cache = bf16[1,2,8,12,384]{4,3,2,1,0:T(8,128)(2,1)} copy(bf16[1,2,8,12,384]{4,2,3,1,0:T(8,128)(2,1)} %param.15) | data formatting | bytes 294912 | tf_op args[4]
  3.9 1.8 %copy.14.held = bf16[1,4,8,12,384]{4,3,2,1,0:T(8,128)(2,1)} copy(bf16[1,4,8,12,384]{4,2,3,1,0:T(8,128)(2,1)} %param.11) | data formatting | bytes 589824 | tf_op args[0]
  5.6 1.8 %copy.15.incoming = bf16[1,4,8,12,384]{4,3,2,1,0:T(8,128)(2,1)} copy(bf16[1,4,8,12,384]{4,2,3,1,0:T(8,128)(2,1)} %param.12) | data formatting | bytes 589824 | tf_op args[1]
  7.4 54.7 %shard_map.130 = (bf16[2,1,4,8,12,384]{5,4,3,2,1,0:T(8,128)(2,1)}, bf16[1,2,8,12,384]{4,3,2,1,0:T(8,128)(2,1)}, bf16[1,2,8,12,384]{4,3,2,1,0:T(8,128)(2,1)}) custom-call(s32[5]{0:T(128)} %counts.1, bf16[1,4,8,12,384]{4,3,2,1,0:T(8,128)(2,1)} %copy.14.held, bf16[1,4,8,12,384]{4,3,2,1,0:T(8,128)(2,1)} %copy.15.incoming, ...), custom_call_target="tpu_custom_call" | custom-call | tf_op jit(solution)/shard_map/pallas_call | solution.py:300
  62.1 2.1 %copy.18 = bf16[2,1,4,8,12,384]{5,3,4,2,1,0:T(8,128)(2,1)} copy(bf16[2,1,4,8,12,384]{5,4,3,2,1,0:T(8,128)(2,1)} %get-tuple-element.3) | data formatting | bytes 1179648 | tf_op jit(solution)/shard_map/pallas_call | solution.py:300
  64.2 1.6 %copy.19 = bf16[1,2,8,12,384]{4,2,3,1,0:T(8,128)(2,1)} copy(bf16[1,2,8,12,384]{4,3,2,1,0:T(8,128)(2,1)} %get-tuple-element.4) | data formatting | bytes 294912 | tf_op jit(solution)/shard_map/pallas_call | solution.py:300
  65.8 1.6 %copy.20 = bf16[1,2,8,12,384]{4,2,3,1,0:T(8,128)(2,1)} copy(bf16[1,2,8,12,384]{4,3,2,1,0:T(8,128)(2,1)} %get-tuple-element.5) | data formatting | bytes 294912 | tf_op jit(solution)/shard_map/pallas_call | solution.py:300
where the time goes:
time: 67.7 us; the launch traced here: 67.4 us
  Pallas kernels  54.7 us (81%)
  local copies, waits for them, and re-layouts  12.1 us (18%)
    pallas_call x1, Pallas kernels, on_device(): pl.pallas_call(kernel, out_shape=(jax.ShapeDtypeStruct((ticks, 1, frames,...  54.7 us
    unnamed x4, local copies, waits for them, and re-layouts  6.76 us
    pallas_call x3, local copies, waits for them, and re-layouts, on_device(): pl.pallas_call(kernel, out_shape=(jax.ShapeDtypeStruct((ticks, 1, frames,...  5.3 us

commit v1 on v0

v1 whole, which is shorter than its diff:
```python
import jax
import jax.numpy as jnp
from jax import lax
from jax.experimental import pallas as pl
from jax.experimental.pallas import tpu as pltpu
from jax.sharding import PartitionSpec as P

EPSILON = 1e-06
MESH = pl.DeviceIdType.MESH


def normed(values, channel_gain):
    factor = lax.rsqrt(jnp.mean(values * values, axis=-1, keepdims=True) + EPSILON)
    half = values * factor * (0.5 * channel_gain)
    return half + half * jnp.tanh(half)


def with_neighbours(values, above, below):
    height = values.shape[1]
    row = lax.broadcasted_iota(jnp.int32, values.shape[:2] + (1,), 1)
    down = jnp.where(row == 0, above, pltpu.roll(values, 1, 1))
    up = jnp.where(row == height - 1, below, pltpu.roll(values, height - 1, 1))
    return down, up


def kernel(
    counts, held, incoming, first_cache, second_cache, first_kernel, first_bias, first_gain,
    second_kernel, second_bias, second_gain, out, first_out, second_out,
    raw, raw_edge, fcache, fcache_edge, scache, scache_edge, second_in, second_edge,
    x1, x2, w1, w2, acc, local_sem, w_sem, send_sem, recv_sem,
):
    ticks, frames, cols, height, channels = (out.shape[i] for i in (0, 2, 3, 4, 5))
    half = frames // 2
    sections, strips = lax.axis_size("segment"), lax.axis_size("strip")
    s, p = lax.axis_index("segment"), lax.axis_index("strip")
    has_above, has_below = p > 0, p < strips - 1
    f32, bf16 = jnp.float32, jnp.bfloat16

    local = [
        pltpu.make_async_copy(held.at[0], raw.at[0], local_sem.at[0]),
        pltpu.make_async_copy(first_cache.at[0], fcache, local_sem.at[1]),
        pltpu.make_async_copy(second_cache.at[0], scache, local_sem.at[2]),
    ]
    for copy in local:
        copy.start()
    fresh = pltpu.make_async_copy(incoming.at[0], raw.at[1], local_sem.at[3])

    def weight(source, target, which, a, b, c):
        return pltpu.make_async_copy(
            source.at[0, a, b, c],
            target.at[pl.ds((a * 3 + b) * channels, channels), pl.ds(c * channels, channels)],
            w_sem.at[which],
        )

    taps = [(a, b, c) for a in range(3) for b in range(3) for c in range(3)]
    around = [(i, j) for i in (-1, 0, 1) for j in (-1, 0, 1) if (i, j) != (0, 0)]
    barrier = pltpu.get_barrier_semaphore()

    def exists(i, j):
        return (s + i >= 0) & (s + i < sections) & (p + j >= 0) & (p + j < strips)

    for i, j in around:
        @pl.when(exists(i, j))
        def _(i=i, j=j):
            pl.semaphore_signal(barrier, inc=1, device_id=(s + i, p + j), device_id_type=MESH)

    for tap in taps:
        weight(first_kernel, w1, 0, *tap).start()

    pl.semaphore_wait(barrier, sum(exists(i, j).astype(jnp.int32) for i, j in around))

    def remote(source, target, k, i, j):
        return pltpu.make_async_remote_copy(
            src_ref=source, dst_ref=target, send_sem=send_sem.at[k], recv_sem=recv_sem.at[k],
            device_id=(s + i, p + j), device_id_type=MESH,
        )

    low, high = pl.ds(0, 2), pl.ds(height - 2, 2)

    def edge(source, target, side, k, i):
        rows, j = (high, 1) if side == 0 else (low, -1)
        return remote(source.at[:, :, rows], target, k + side, i, j)

    def start_edges(side):
        return [
            edge(first_cache.at[0], fcache_edge.at[side], side, 2, 0),
            edge(held.at[0], raw_edge.at[0, side], side, 0, 0),
            edge(second_cache.at[0], scache_edge.at[side], side, 4, 0),
        ]

    def fresh_edge(side):
        return edge(incoming.at[0], raw_edge.at[1, side], side, 6, 0)

    def span(h):
        return pl.ds(h * half, half)

    def block(h):
        return remote(out.at[0, 0, span(h)], raw.at[1, span(h)], 8 + h, 1, 0)

    def block_edge(h, side):
        target = raw_edge.at[1, side, span(h)]
        return edge(out.at[0, 0, span(h)], target, side, 10 + 2 * h, 1)

    def second_rows(tick, h, side):
        target = second_edge.at[tick, side, span(h)]
        return edge(second_in.at[tick, span(h)], target, side, 14 + 4 * tick + 2 * h, 0)

    sends_to = (has_below, has_above)
    takes_from = (has_above, has_below)
    for side in range(2):
        @pl.when(sends_to[side])
        def _(side=side):
            for copy in start_edges(side):
                copy.start()

    @pl.when(s == 0)
    def _():
        fresh.start()
        for side in range(2):
            @pl.when(sends_to[side])
            def _(side=side):
                fresh_edge(side).start()

    for tap in taps:
        weight(second_kernel, w2, 1, *tap).start()

    acc[:, 0] = jnp.zeros((half, height, 3 * channels), f32)
    acc[:, cols + 1] = jnp.zeros((half, height, 3 * channels), f32)
    for side in range(2):
        @pl.when(jnp.logical_not(takes_from[side]))
        def _(side=side):
            raw_edge[:, side] = jnp.zeros((ticks, frames, cols, 2, channels), bf16)
            second_edge[:, side] = jnp.zeros((ticks, frames, cols, 2, channels), bf16)
            fcache_edge[side] = jnp.zeros((2, cols, 2, channels), bf16)
            scache_edge[side] = jnp.zeros((2, cols, 2, channels), bf16)

    def put(window, f, b, values):
        flat = values.reshape(cols * height, channels).astype(bf16)
        window[f, :, b * channels : (b + 1) * channels] = flat

    def edges_of(ref_above, ref_below):
        shape = (cols, 2, channels)
        which = lax.broadcasted_iota(jnp.int32, shape, 1)
        return jnp.where(which == 1, ref_above.astype(f32), ref_below.astype(f32))

    for copy in local:
        copy.wait()
    for side in range(2):
        @pl.when(takes_from[side])
        def _(side=side):
            for copy in start_edges(side):
                copy.wait_recv()

    for window, cache, rows in ((x1, fcache, fcache_edge), (x2, scache, scache_edge)):
        for f in range(2):
            values = cache[f].astype(f32)
            pair = edges_of(rows[0, f], rows[1, f])
            down, up = with_neighbours(values, pair[:, 1:2], pair[:, 0:1])
            for b, shifted in enumerate((down, values, up)):
                put(window, f, b, shifted)

    def convolve(window, weights, h):
        lhs = jnp.concatenate(
            [
                window[pl.ds(h * half + a, half)].reshape(half * cols * height, 3 * channels)
                for a in range(3)
            ],
            axis=-1,
        )
        product = jnp.dot(lhs, weights[...], preferred_element_type=f32)
        acc[:, 1 : cols + 1] = product.reshape(half, cols, height, 3 * channels)

    def summed(f, bias):
        return (
            acc[f, 0:cols, :, 0:channels]
            + acc[f, 1 : cols + 1, :, channels : 2 * channels]
            + acc[f, 2 : cols + 2, :, 2 * channels : 3 * channels]
            + bias
        )

    @pl.loop(0, ticks)
    def _(tick):
        live = counts[sections - 1 - s + tick]

        @pl.loop(0, 2)
        def _(h):
            @pl.when((tick > 0) & (s == 0) & (h == 0))
            def _():
                fresh.wait()
                for side in range(2):
                    @pl.when(takes_from[side])
                    def _(side=side):
                        fresh_edge(side).wait_recv()

            @pl.when((tick > 0) & (s > 0))
            def _():
                block(h).wait_recv()
                for side in range(2):
                    @pl.when(takes_from[side])
                    def _(side=side):
                        block_edge(h, side).wait_recv()

            @pl.loop(0, half)
            def _(i):
                f = h * half + i
                alive = f < live
                values = normed(jnp.where(alive, raw[tick, f].astype(f32), 0.0), first_gain[...])
                pair = edges_of(raw_edge[tick, 0, f], raw_edge[tick, 1, f])
                pair = normed(jnp.where(alive, pair, 0.0), first_gain[...])
                down, up = with_neighbours(values, pair[:, 1:2], pair[:, 0:1])
                for b, shifted in enumerate((down, values, up)):
                    put(x1, 2 + f, b, shifted)

            @pl.when((tick == 0) & (h == 0))
            def _():
                for tap in taps:
                    weight(first_kernel, w1, 0, *tap).wait()

            convolve(x1, w1, h)

            @pl.loop(0, half)
            def _(i):
                f = h * half + i
                hidden = jnp.where(f < live, summed(i, first_bias[...]), 0.0)
                values = normed(hidden, second_gain[...])
                second_in[tick, f] = values.astype(bf16)
                put(x2, 2 + f, 1, values)

            for side in range(2):
                @pl.when(sends_to[side])
                def _(side=side):
                    second_rows(tick, h, side).start()

        @pl.loop(0, 2)
        def _(h):
            for side in range(2):
                @pl.when(takes_from[side])
                def _(side=side):
                    second_rows(tick, h, side).wait_recv()

            @pl.loop(0, half)
            def _(i):
                f = h * half + i
                values = second_in[tick, f].astype(f32)
                pair = edges_of(second_edge[tick, 0, f], second_edge[tick, 1, f])
                down, up = with_neighbours(values, pair[:, 1:2], pair[:, 0:1])
                put(x2, 2 + f, 0, down)
                put(x2, 2 + f, 2, up)

            @pl.when((tick == 0) & (h == 0))
            def _():
                for tap in taps:
                    weight(second_kernel, w2, 1, *tap).wait()

            convolve(x2, w2, h)

            @pl.loop(0, half)
            def _(i):
                f = h * half + i
                total = summed(i, second_bias[...]) + raw[tick, f].astype(f32)
                out[tick, 0, f] = jnp.where(f < live, total, 0.0).astype(bf16)

            @pl.when((tick == 0) & (s < sections - 1))
            def _():
                block(h).start()
                for side in range(2):
                    @pl.when(sends_to[side])
                    def _(side=side):
                        block_edge(h, side).start()

        for window in (x1, x2):
            for j in range(2):
                window[j] = window[live + j]

    for window, target in ((x1, first_out), (x2, second_out)):
        for j in range(2):
            values = window[j, :, channels : 2 * channels].astype(f32)
            target[0, j] = values.reshape(cols, height, channels).astype(bf16)

    for side in range(2):
        @pl.when(sends_to[side])
        def _(side=side):
            for copy in start_edges(side):
                copy.wait_send()

            @pl.loop(0, ticks)
            def _(tick):
                for h in range(2):
                    second_rows(tick, h, side).wait_send()

            @pl.when(s == 0)
            def _():
                fresh_edge(side).wait_send()

            @pl.when(s < sections - 1)
            def _():
                for h in range(2):
                    block_edge(h, side).wait_send()

    @pl.when(s < sections - 1)
    def _():
        for h in range(2):
            block(h).wait_send()


def deliver(*refs):
    sem = refs[-1]
    copies = [
        pltpu.make_async_copy(refs[k], refs[3 + k], sem.at[k]) for k in range(3)
    ]
    for copy in copies:
        copy.start()
    for copy in copies:
        copy.wait()


def swapped(array):
    return jnp.swapaxes(array, -3, -2)


def on_device(
    held_blocks, incoming, frame_counts, first_cache, second_cache, first_kernel, first_bias,
    first_gain, second_kernel, second_bias, second_gain,
):
    held_blocks, incoming, first_cache, second_cache = (
        swapped(v) for v in (held_blocks, incoming, first_cache, second_cache)
    )
    _, frames, cols, height, channels = held_blocks.shape
    ticks = incoming.shape[0] + 1
    bf16 = jnp.bfloat16
    anywhere = pl.BlockSpec(memory_space=pltpu.HBM)
    inside = pl.BlockSpec(memory_space=pltpu.VMEM)
    shapes = (
        jax.ShapeDtypeStruct((ticks, 1, frames, cols, height, channels), bf16),
        jax.ShapeDtypeStruct(first_cache.shape, bf16),
        jax.ShapeDtypeStruct(second_cache.shape, bf16),
    )
    transfers = 14 + 4 * ticks
    results = pl.pallas_call(
        kernel,
        out_shape=shapes,
        in_specs=[pl.BlockSpec(memory_space=pltpu.SMEM)] + [anywhere] * 5
        + [inside, inside, anywhere, inside, inside],
        out_specs=(inside, inside, inside),
        scratch_shapes=[
            pltpu.VMEM((ticks, frames, cols, height, channels), bf16),
            pltpu.VMEM((ticks, 2, frames, cols, 2, channels), bf16),
            pltpu.VMEM((2, cols, height, channels), bf16),
            pltpu.VMEM((2, 2, cols, 2, channels), bf16),
            pltpu.VMEM((2, cols, height, channels), bf16),
            pltpu.VMEM((2, 2, cols, 2, channels), bf16),
            pltpu.VMEM((ticks, frames, cols, height, channels), bf16),
            pltpu.VMEM((ticks, 2, frames, cols, 2, channels), bf16),
            pltpu.VMEM((frames + 2, cols * height, 3 * channels), bf16),
            pltpu.VMEM((frames + 2, cols * height, 3 * channels), bf16),
            pltpu.VMEM((9 * channels, 3 * channels), bf16),
            pltpu.VMEM((9 * channels, 3 * channels), bf16),
            pltpu.VMEM((frames // 2, cols + 2, height, 3 * channels), jnp.float32),
            pltpu.SemaphoreType.DMA((4,)),
            pltpu.SemaphoreType.DMA((2,)),
            pltpu.SemaphoreType.DMA((transfers,)),
            pltpu.SemaphoreType.DMA((transfers,)),
        ],
        compiler_params=pltpu.CompilerParams(
            collective_id=0, has_side_effects=True, vmem_limit_bytes=60 * 1024 * 1024
        ),
    )(
        frame_counts, held_blocks, incoming, first_cache, second_cache, first_kernel, first_bias,
        first_gain, second_kernel, second_bias, second_gain,
    )
    results = pl.pallas_call(
        deliver,
        out_shape=shapes,
        in_specs=[inside] * 3,
        out_specs=(anywhere,) * 3,
        scratch_shapes=[pltpu.SemaphoreType.DMA((3,))],
        compiler_params=pltpu.CompilerParams(vmem_limit_bytes=4 * 1024 * 1024),
    )(*results)
    return tuple(swapped(v) for v in results)


def solution(mesh):
    return jax.shard_map(
        on_device,
        mesh=mesh,
        in_specs=(
            P("segment", None, "strip", None, None),
            P(None, None, "strip", None, None),
            P(),
            P("segment", None, "strip", None, None),
            P("segment", None, "strip", None, None),
            P("segment", None, None, None, None, None),
            P("segment", None),
            P("segment", None),
            P("segment", None, None, None, None, None),
            P("segment", None),
            P("segment", None),
        ),
        out_specs=(
            P(None, "segment", None, "strip", None, None),
            P("segment", None, "strip", None, None),
            P("segment", None, "strip", None, None),
        ),
        check_vma=False,
    )
```

time: 67.7 us -> 42.4 us (0.63)
  the two profiles are of different devices: /device:TPU:18 before, /device:TPU:0 now
where the time goes in v1:
time: 42.4 us; the launch traced here: 42.2 us
  Pallas kernels  38.7 us (91%)
  local copies, waits for them, and re-layouts  2.88 us (7%)
  between operations  0.65 us (2%)
    pallas_call x1, Pallas kernels, on_device(): pl.pallas_call(kernel, out_shape=shapes, in_specs=[pl.BlockSpec(memory_sp...  37.7 us
    unnamed x6, local copies, waits for them, and re-layouts  2.88 us
    pallas_call x1, Pallas kernels, on_device(): pl.pallas_call(deliver, out_shape=shapes, in_specs=[inside] * 3, out_spec...  0.93 us

profile of v1, /device:TPU:0, one launch (start us, length us, event | category | flops | bytes accessed | tf_op | source)
XLA Modules:
  0.0 42.2 jit_solution(1607602842551651418)
XLA Ops:
  0.6 37.7 %shard_map.130 = (bf16[2,1,4,12,8,384]{5,4,3,2,1,0:T(8,128)(2,1)}, bf16[1,2,12,8,384]{4,3,2,1,0:T(8,128)(2,1)}, bf16[1,2,12,8,384]{4,3,2,1,0:T(8,128)(2,1)}) custom-call(s32[5]{0:T(128)} %counts.1, bf16[1,4,12,8,384]{4,3,2,1,0:T(8,128)(2,1)} %bitcast.7, bf16[1,4,12,8,384]{4,3,2,1,0:T(8,128)(2,1)} %bitcast.8, bf16[1,2,12,8,384]{4,3,2,1,0:T(8,128)(2,1)} %bitcast.9, ...), custom_call_target="tpu_custom_call" | custom-call | tf_op jit(solution)/shard_map/pallas_call | solution.py:339
  38.4 0.0 copy-start
  38.4 1.1 %copy-done = bf16[2,1,4,12,8,384]{5,4,3,2,1,0:T(8,128)(2,1)S(1)} copy-done((bf16[2,1,4,12,8,384]{5,4,3,2,1,0:T(8,128)(2,1)S(1)}, bf16[2,1,4,12,8,384]{5,4,3,2,1,0:T(8,128)(2,1)}, u32[]{:S(2)}) %copy-start) | copy-done | bytes 589848
  39.4 0.0 copy-start.1
  39.4 0.9 %copy-done.1 = bf16[1,2,12,8,384]{4,3,2,1,0:T(8,128)(2,1)S(1)} copy-done((bf16[1,2,12,8,384]{4,3,2,1,0:T(8,128)(2,1)S(1)}, bf16[1,2,12,8,384]{4,3,2,1,0:T(8,128)(2,1)}, u32[]{:S(2)}) %copy-start.1) | copy-done | bytes 147480
  40.3 0.0 copy-start.2
  40.4 0.9 %copy-done.2 = bf16[1,2,12,8,384]{4,3,2,1,0:T(8,128)(2,1)S(1)} copy-done((bf16[1,2,12,8,384]{4,3,2,1,0:T(8,128)(2,1)S(1)}, bf16[1,2,12,8,384]{4,3,2,1,0:T(8,128)(2,1)}, u32[]{:S(2)}) %copy-start.2) | copy-done | bytes 147480
  41.3 0.9 %shard_map.131 = (bf16[2,1,4,12,8,384]{5,4,3,2,1,0:T(8,128)(2,1)}, bf16[1,2,12,8,384]{4,3,2,1,0:T(8,128)(2,1)}, bf16[1,2,12,8,384]{4,3,2,1,0:T(8,128)(2,1)}) custom-call(bf16[2,1,4,12,8,384]{5,4,3,2,1,0:T(8,128)(2,1)S(1)} %copy-done, bf16[1,2,12,8,384]{4,3,2,1,0:T(8,128)(2,1)S(1)} %copy-done.1, bf16[1,2,12,8,384]{4,3,2,1,0:T(8,128)(2,1)S(1)} %copy-done.2), custom_call_target="tpu_custom_call" | custom-call | tf_op jit(solution)/shard_map/pallas_call | solution.py:371
Async XLA Ops:
  38.4 1.1 %copy-start = (bf16[2,1,4,12,8,384]{5,4,3,2,1,0:T(8,128)(2,1)S(1)}, bf16[2,1,4,12,8,384]{5,4,3,2,1,0:T(8,128)(2,1)}, u32[]{:S(2)}) copy-start(bf16[2,1,4,12,8,384]{5,4,3,2,1,0:T(8,128)(2,1)} %get-tuple-element.9.refs_0_) | copy-start | bytes 1769476
  39.4 0.9 %copy-start.1 = (bf16[1,2,12,8,384]{4,3,2,1,0:T(8,128)(2,1)S(1)}, bf16[1,2,12,8,384]{4,3,2,1,0:T(8,128)(2,1)}, u32[]{:S(2)}) copy-start(bf16[1,2,12,8,384]{4,3,2,1,0:T(8,128)(2,1)} %get-tuple-element.10.refs_1_) | copy-start | bytes 442372
  40.3 0.9 %copy-start.2 = (bf16[1,2,12,8,384]{4,3,2,1,0:T(8,128)(2,1)S(1)}, bf16[1,2,12,8,384]{4,3,2,1,0:T(8,128)(2,1)}, u32[]{:S(2)}) copy-start(bf16[1,2,12,8,384]{4,3,2,1,0:T(8,128)(2,1)} %get-tuple-element.11.refs_2_) | copy-start | bytes 442372

commit v2 on v1

--- a/solution.py
+++ b/solution.py
@@ -45,14 +45,27 @@
         copy.start()
     fresh = pltpu.make_async_copy(incoming.at[0], raw.at[1], local_sem.at[3])
 
-    def weight(source, target, which, a, b, c):
-        return pltpu.make_async_copy(
-            source.at[0, a, b, c],
-            target.at[pl.ds((a * 3 + b) * channels, channels), pl.ds(c * channels, channels)],
-            w_sem.at[which],
-        )
-
-    taps = [(a, b, c) for a in range(3) for b in range(3) for c in range(3)]
+    def weights(source, target, which, blocks, start):
+        return [
+            pltpu.make_async_copy(
+                source.at[0, a, b, c],
+                target.at[pl.ds((start + k) * channels, channels), pl.ds(c * channels, channels)],
+                w_sem.at[which],
+            )
+            for k, (a, b) in enumerate(blocks)
+            for c in range(3)
+        ]
+
+    first_a = [(0, 1), (1, 1), (2, 1)]
+    first_b = [(a, b) for a in range(3) for b in (0, 2)]
+    second_a = [(0, 1), (0, 0), (0, 2), (1, 1), (2, 1)]
+    second_b = [(a, b) for a in (1, 2) for b in (0, 2)]
+    loads = [
+        weights(first_kernel, w1, 0, first_a, 0),
+        weights(first_kernel, w1, 1, first_b, len(first_a)),
+        weights(second_kernel, w2, 2, second_a, 0),
+        weights(second_kernel, w2, 3, second_b, len(second_a)),
+    ]
     around = [(i, j) for i in (-1, 0, 1) for j in (-1, 0, 1) if (i, j) != (0, 0)]
     barrier = pltpu.get_barrier_semaphore()
 
@@ -64,8 +77,8 @@
         def _(i=i, j=j):
             pl.semaphore_signal(barrier, inc=1, device_id=(s + i, p + j), device_id_type=MESH)
 
-    for tap in taps:
-        weight(first_kernel, w1, 0, *tap).start()
+    for copy in loads[0]:
+        copy.start()
 
     pl.semaphore_wait(barrier, sum(exists(i, j).astype(jnp.int32) for i, j in around))
 
@@ -121,11 +134,12 @@
             def _(side=side):
                 fresh_edge(side).start()
 
-    for tap in taps:
-        weight(second_kernel, w2, 1, *tap).start()
-
-    acc[:, 0] = jnp.zeros((half, height, 3 * channels), f32)
-    acc[:, cols + 1] = jnp.zeros((half, height, 3 * channels), f32)
+    for copy in loads[1]:
+        copy.start()
+
+    for h in range(2):
+        for at in (0, cols + 1):
+            acc[h, :, at] = jnp.zeros((half, height, 3 * channels), f32)
     for side in range(2):
         @pl.when(jnp.logical_not(takes_from[side]))
         def _(side=side):
@@ -134,47 +148,43 @@
             fcache_edge[side] = jnp.zeros((2, cols, 2, channels), bf16)
             scache_edge[side] = jnp.zeros((2, cols, 2, channels), bf16)
 
-    def put(window, f, b, values):
+    def put(window, f, plane, values):
         flat = values.reshape(cols * height, channels).astype(bf16)
-        window[f, :, b * channels : (b + 1) * channels] = flat
-
-    def edges_of(ref_above, ref_below):
-        shape = (cols, 2, channels)
-        which = lax.broadcasted_iota(jnp.int32, shape, 1)
-        return jnp.where(which == 1, ref_above.astype(f32), ref_below.astype(f32))
+        window[f, :, plane * channels : (plane + 1) * channels] = flat
+
+    def put_shifted(window, f, above, below, prepare):
+        values = window[f, :, 0:channels].astype(f32).reshape(cols, height, channels)
+        which = lax.broadcasted_iota(jnp.int32, (cols, 2, channels), 1)
+        pair = prepare(jnp.where(which == 1, above.astype(f32), below.astype(f32)))
+        down, up = with_neighbours(values, pair[:, 1:2], pair[:, 0:1])
+        put(window, f, 1, down)
+        put(window, f, 2, up)
 
     for copy in local:
         copy.wait()
-    for side in range(2):
-        @pl.when(takes_from[side])
-        def _(side=side):
-            for copy in start_edges(side):
-                copy.wait_recv()
-
-    for window, cache, rows in ((x1, fcache, fcache_edge), (x2, scache, scache_edge)):
+    for window, cache in ((x1, fcache), (x2, scache)):
         for f in range(2):
-            values = cache[f].astype(f32)
-            pair = edges_of(rows[0, f], rows[1, f])
-            down, up = with_neighbours(values, pair[:, 1:2], pair[:, 0:1])
-            for b, shifted in enumerate((down, values, up)):
-                put(window, f, b, shifted)
-
-    def convolve(window, weights, h):
+            put(window, f, 0, cache[f].astype(f32))
+
+    def part(window, matrix, h, pieces, start):
         lhs = jnp.concatenate(
             [
-                window[pl.ds(h * half + a, half)].reshape(half * cols * height, 3 * channels)
-                for a in range(3)
+                window[pl.ds(h * half + a, half), :, first * channels : last * channels].reshape(
+                    half * cols * height, (last - first) * channels
+                )
+                for a, first, last in pieces
             ],
             axis=-1,
         )
-        product = jnp.dot(lhs, weights[...], preferred_element_type=f32)
-        acc[:, 1 : cols + 1] = product.reshape(half, cols, height, 3 * channels)
-
-    def summed(f, bias):
+        rows = matrix[start * channels : start * channels + lhs.shape[-1]]
+        product = jnp.dot(lhs, rows, preferred_element_type=f32)
+        return product.reshape(half, cols, height, 3 * channels)
+
+    def summed(h, f, bias):
         return (
-            acc[f, 0:cols, :, 0:channels]
-            + acc[f, 1 : cols + 1, :, channels : 2 * channels]
-            + acc[f, 2 : cols + 2, :, 2 * channels : 3 * channels]
+            acc[h, f, 0:cols, :, 0:channels]
+            + acc[h, f, 1 : cols + 1, :, channels : 2 * channels]
+            + acc[h, f, 2 : cols + 2, :, 2 * channels : 3 * channels]
             + bias
         )
 
@@ -182,11 +192,48 @@
     def _(tick):
         live = counts[sections - 1 - s + tick]
 
-        @pl.loop(0, 2)
-        def _(h):
+        def first_start(h):
             @pl.when((tick > 0) & (s == 0) & (h == 0))
             def _():
                 fresh.wait()
+
+            @pl.when((tick > 0) & (s > 0))
+            def _():
+                block(h).wait_recv()
+
+            @pl.loop(0, half)
+            def _(i):
+                f = h * half + i
+                values = jnp.where(f < live, raw[tick, f].astype(f32), 0.0)
+                put(x1, 2 + f, 0, normed(values, first_gain[...]))
+
+            @pl.when((tick == 0) & (h == 0))
+            def _():
+                for copy in loads[0]:
+                    copy.wait()
+                for copy in loads[2] + loads[3]:
+                    copy.start()
+
+            acc[h, :, 1 : cols + 1] = part(x1, w1, h, [(a, 0, 1) for a in range(3)], 0)
+
+        def first_end(h):
+            @pl.when((tick == 0) & (h == 0))
+            def _():
+                for side in range(2):
+                    @pl.when(takes_from[side])
+                    def _(side=side):
+                        for copy in start_edges(side):
+                            copy.wait_recv()
+
+                for window, rows in ((x1, fcache_edge), (x2, scache_edge)):
+                    for f in range(2):
+                        put_shifted(window, f, rows[0, f], rows[1, f], lambda pair: pair)
+
+                for copy in loads[1]:
+                    copy.wait()
+
+            @pl.when((tick > 0) & (s == 0) & (h == 0))
+            def _():
                 for side in range(2):
                     @pl.when(takes_from[side])
                     def _(side=side):
@@ -194,7 +241,6 @@
 
             @pl.when((tick > 0) & (s > 0))
             def _():
-                block(h).wait_recv()
                 for side in range(2):
                     @pl.when(takes_from[side])
                     def _(side=side):
@@ -203,36 +249,50 @@
             @pl.loop(0, half)
             def _(i):
                 f = h * half + i
-                alive = f < live
-                values = normed(jnp.where(alive, raw[tick, f].astype(f32), 0.0), first_gain[...])
-                pair = edges_of(raw_edge[tick, 0, f], raw_edge[tick, 1, f])
-                pair = normed(jnp.where(alive, pair, 0.0), first_gain[...])
-                down, up = with_neighbours(values, pair[:, 1:2], pair[:, 0:1])
-                for b, shifted in enumerate((down, values, up)):
-                    put(x1, 2 + f, b, shifted)
-
-            @pl.when((tick == 0) & (h == 0))
-            def _():
-                for tap in taps:
-                    weight(first_kernel, w1, 0, *tap).wait()
-
-            convolve(x1, w1, h)
+                put_shifted(
+                    x1, 2 + f, raw_edge[tick, 0, f], raw_edge[tick, 1, f],
+                    lambda pair: normed(jnp.where(f < live, pair, 0.0), first_gain[...]),
+                )
+
+            acc[h, :, 1 : cols + 1] += part(
+                x1, w1, h, [(a, 1, 3) for a in range(3)], len(first_a)
+            )
 
             @pl.loop(0, half)
             def _(i):
                 f = h * half + i
-                hidden = jnp.where(f < live, summed(i, first_bias[...]), 0.0)
+                hidden = jnp.where(f < live, summed(h, i, first_bias[...]), 0.0)
                 values = normed(hidden, second_gain[...])
                 second_in[tick, f] = values.astype(bf16)
-                put(x2, 2 + f, 1, values)
+                put(x2, 2 + f, 0, values)
 
             for side in range(2):
                 @pl.when(sends_to[side])
                 def _(side=side):
                     second_rows(tick, h, side).start()
 
+        @pl.loop(0, 4)
+        def _(slot):
+            ending = jnp.where(tick == 0, slot // 2, slot % 2)
+            h = jnp.where(tick == 0, slot % 2, slot // 2)
+
+            @pl.when(ending == 0)
+            def _():
+                first_start(h)
+
+            @pl.when(ending == 1)
+            def _():
+                first_end(h)
+
         @pl.loop(0, 2)
         def _(h):
+            @pl.when((tick == 0) & (h == 0))
+            def _():
+                for copy in loads[2]:
+                    copy.wait()
+
+            acc[h, :, 1 : cols + 1] = part(x2, w2, h, [(0, 0, 3), (1, 0, 1), (2, 0, 1)], 0)
+
             for side in range(2):
                 @pl.when(takes_from[side])
                 def _(side=side):
@@ -241,23 +301,21 @@
             @pl.loop(0, half)
             def _(i):
                 f = h * half + i
-                values = second_in[tick, f].astype(f32)
-                pair = edges_of(second_edge[tick, 0, f], second_edge[tick, 1, f])
-                down, up = with_neighbours(values, pair[:, 1:2], pair[:, 0:1])
-                put(x2, 2 + f, 0, down)
-                put(x2, 2 + f, 2, up)
+                put_shifted(
+                    x2, 2 + f, second_edge[tick, 0, f], second_edge[tick, 1, f], lambda pair: pair
+                )
 
             @pl.when((tick == 0) & (h == 0))
             def _():
-                for tap in taps:
-                    weight(second_kernel, w2, 1, *tap).wait()
-
-            convolve(x2, w2, h)
+                for copy in loads[3]:
+                    copy.wait()
+
+            acc[h, :, 1 : cols + 1] += part(x2, w2, h, [(1, 1, 3), (2, 1, 3)], len(second_a))
 
             @pl.loop(0, half)
             def _(i):
                 f = h * half + i
-                total = summed(i, second_bias[...]) + raw[tick, f].astype(f32)
+                total = summed(h, i, second_bias[...]) + raw[tick, f].astype(f32)
                 out[tick, 0, f] = jnp.where(f < live, total, 0.0).astype(bf16)
 
             @pl.when((tick == 0) & (s < sections - 1))
@@ -274,7 +332,7 @@
 
     for window, target in ((x1, first_out), (x2, second_out)):
         for j in range(2):
-            values = window[j, :, channels : 2 * channels].astype(f32)
+            values = window[j, :, 0:channels].astype(f32)
             target[0, j] = values.reshape(cols, height, channels).astype(bf16)
 
     for side in range(2):
@@ -338,7 +396,7 @@
     transfers = 14 + 4 * ticks
     results = pl.pallas_call(
         kernel,
-        out_shape=shapes,
+        out_shape=tuple(pltpu.VMEM(v.shape, v.dtype) for v in shapes),
         in_specs=[pl.BlockSpec(memory_space=pltpu.SMEM)] + [anywhere] * 5
         + [inside, inside, anywhere, inside, inside],
         out_specs=(inside, inside, inside),
@@ -355,9 +413,9 @@
             pltpu.VMEM((frames + 2, cols * height, 3 * channels), bf16),
             pltpu.VMEM((9 * channels, 3 * channels), bf16),
             pltpu.VMEM((9 * channels, 3 * channels), bf16),
-            pltpu.VMEM((frames // 2, cols + 2, height, 3 * channels), jnp.float32),
+            pltpu.VMEM((2, frames // 2, cols + 2, height, 3 * channels), jnp.float32),
             pltpu.SemaphoreType.DMA((4,)),
-            pltpu.SemaphoreType.DMA((2,)),
+            pltpu.SemaphoreType.DMA((4,)),
             pltpu.SemaphoreType.DMA((transfers,)),
             pltpu.SemaphoreType.DMA((transfers,)),
         ],

time: 42.4 us -> 36.5 us (0.86)
  Pallas kernels: 38.7 us -> 35.7 us
  local copies, waits for them, and re-layouts: 2.88 us -> 0 us
    pallas_call x1, Pallas kernels: 37.7 us -> 34.7 us  [on_device(): pl.pallas_call(kernel, out_shape=tuple((pltpu.VMEM(v.shape, v.dtype) for...]
    unnamed x6 -> x0, local copies, waits for them, and re-layouts: 2.88 us -> none
where the time goes in v2:
time: 36.5 us; the launch traced here: 36.3 us
  Pallas kernels  35.7 us (98%)
  between operations  0.64 us (2%)
    pallas_call x1, Pallas kernels, on_device(): pl.pallas_call(kernel, out_shape=tuple((pltpu.VMEM(v.shape, v.dtype) for...  34.7 us
    pallas_call x1, Pallas kernels, on_device(): pl.pallas_call(deliver, out_shape=shapes, in_specs=[inside] * 3, out_spec...  0.93 us

profile of v2, /device:TPU:0, one launch (start us, length us, event | category | flops | bytes accessed | tf_op | source)
XLA Modules:
  0.0 36.3 jit_solution(17356584054492383430)
XLA Ops:
  0.6 34.7 %shard_map.130 = (bf16[2,1,4,12,8,384]{5,4,3,2,1,0:T(8,128)(2,1)S(1)}, bf16[1,2,12,8,384]{4,3,2,1,0:T(8,128)(2,1)S(1)}, bf16[1,2,12,8,384]{4,3,2,1,0:T(8,128)(2,1)S(1)}) custom-call(s32[5]{0:T(128)} %counts.1, bf16[1,4,12,8,384]{4,3,2,1,0:T(8,128)(2,1)} %bitcast.7, bf16[1,4,12,8,384]{4,3,2,1,0:T(8,128)(2,1)} %bitcast.8, bf16[1,2,12,8,384]{4,3,2,1,0:T(8,128)(2,1)} %bitcast.9, ...), custom_call_target="tpu_custom_call" | custom-call | tf_op jit(solution)/shard_map/pallas_call | solution.py:397
  35.4 0.9 %shard_map.131 = (bf16[2,1,4,12,8,384]{5,4,3,2,1,0:T(8,128)(2,1)}, bf16[1,2,12,8,384]{4,3,2,1,0:T(8,128)(2,1)}, bf16[1,2,12,8,384]{4,3,2,1,0:T(8,128)(2,1)}) custom-call(bf16[2,1,4,12,8,384]{5,4,3,2,1,0:T(8,128)(2,1)S(1)} %get-tuple-element.9.refs_0_, bf16[1,2,12,8,384]{4,3,2,1,0:T(8,128)(2,1)S(1)} %get-tuple-element.10.refs_1_, ...), custom_call_target="tpu_custom_call" | custom-call | tf_op jit(solution)/shard_map/pallas_call | solution.py:429

commit v3 on v2

--- a/solution.py
+++ b/solution.py
@@ -26,7 +26,7 @@
 def kernel(
     counts, held, incoming, first_cache, second_cache, first_kernel, first_bias, first_gain,
     second_kernel, second_bias, second_gain, out, first_out, second_out,
-    raw, raw_edge, fcache, fcache_edge, scache, scache_edge, second_in, second_edge,
+    raw, raw_edge, fcache, fcache_edge, scache, scache_edge, second_edge, packed, second_packed,
     x1, x2, w1, w2, acc, local_sem, w_sem, send_sem, recv_sem,
 ):
     ticks, frames, cols, height, channels = (out.shape[i] for i in (0, 2, 3, 4, 5))
@@ -80,59 +80,87 @@
     for copy in loads[0]:
         copy.start()
 
-    pl.semaphore_wait(barrier, sum(exists(i, j).astype(jnp.int32) for i, j in around))
-
     def remote(source, target, k, i, j):
         return pltpu.make_async_remote_copy(
             src_ref=source, dst_ref=target, send_sem=send_sem.at[k], recv_sem=recv_sem.at[k],
             device_id=(s + i, p + j), device_id_type=MESH,
         )
 
-    low, high = pl.ds(0, 2), pl.ds(height - 2, 2)
-
     def edge(source, target, side, k, i):
-        rows, j = (high, 1) if side == 0 else (low, -1)
-        return remote(source.at[:, :, rows], target, k + side, i, j)
-
-    def start_edges(side):
-        return [
-            edge(first_cache.at[0], fcache_edge.at[side], side, 2, 0),
-            edge(held.at[0], raw_edge.at[0, side], side, 0, 0),
-            edge(second_cache.at[0], scache_edge.at[side], side, 4, 0),
-        ]
-
-    def fresh_edge(side):
-        return edge(incoming.at[0], raw_edge.at[1, side], side, 6, 0)
+        rows = pl.ds(side * half, half)
+        return remote(source.at[side], target.at[:, rows], k + side, i, 1 - 2 * side)
+
+    edge_targets = [
+        fcache_edge, raw_edge.at[0, 0], raw_edge.at[0, 1], scache_edge, raw_edge.at[1, 0],
+        raw_edge.at[1, 1],
+    ]
+
+    def start_edge(kind, side):
+        return edge(packed.at[kind], edge_targets[kind], side, 2 * kind, 0)
+
+    def pack(target, frames_of):
+        height_row = lax.broadcasted_iota(jnp.int32, (cols, height, 1), 1)
+        for side in range(2):
+            rows = None
+            for k, values in enumerate(frames_of):
+                shift = (k + 1 - side) % height
+                moved = pltpu.roll(values, shift, 1) if shift else values
+                rows = moved if rows is None else jnp.where(height_row == k, moved, rows)
+            target[side] = rows[:, 0:half].astype(bf16)
 
     def span(h):
         return pl.ds(h * half, half)
 
     def block(h):
-        return remote(out.at[0, 0, span(h)], raw.at[1, span(h)], 8 + h, 1, 0)
+        return remote(out.at[0, 0, span(h)], raw.at[1, span(h)], 12 + h, 1, 0)
 
     def block_edge(h, side):
-        target = raw_edge.at[1, side, span(h)]
-        return edge(out.at[0, 0, span(h)], target, side, 10 + 2 * h, 1)
+        return edge(packed.at[6 + h], raw_edge.at[1, h], side, 14 + 2 * h, 1)
 
     def second_rows(tick, h, side):
-        target = second_edge.at[tick, side, span(h)]
-        return edge(second_in.at[tick, span(h)], target, side, 14 + 4 * tick + 2 * h, 0)
+        k = 18 + 4 * tick + 2 * h
+        return edge(second_packed.at[tick, h], second_edge.at[tick, h], side, k, 0)
 
     sends_to = (has_below, has_above)
     takes_from = (has_above, has_below)
+
+    def each_side(existing, act):
+        for side in range(2):
+            @pl.when(existing[side])
+            def _(side=side):
+                act(side)
+
+    def pack_start(kind):
+        source = {0: fcache, 1: raw.at[0, span(0)], 2: raw.at[0, span(1)], 3: scache}[kind]
+        pack(packed.at[kind], [source[k].astype(f32) for k in range(half)])
+
     for side in range(2):
-        @pl.when(sends_to[side])
+        @pl.when(jnp.logical_not(takes_from[side]))
         def _(side=side):
-            for copy in start_edges(side):
-                copy.start()
+            rows = slice(side * half, (side + 1) * half)
+            zeros = jnp.zeros((cols, half, channels), bf16)
+            fcache_edge[:, rows] = zeros
+            scache_edge[:, rows] = zeros
+            for tick in range(ticks):
+                for h in range(2):
+                    raw_edge[tick, h, :, rows] = zeros
+                    second_edge[tick, h, :, rows] = zeros
+
+    for copy in local:
+        copy.wait()
+    pack_start(0)
+    pack_start(1)
+    pl.semaphore_wait(barrier, sum(exists(i, j).astype(jnp.int32) for i, j in around))
+    for kind in range(2):
+        each_side(sends_to, lambda side: start_edge(kind, side).start())
+    pack_start(2)
+    pack_start(3)
+    for kind in range(2, 4):
+        each_side(sends_to, lambda side: start_edge(kind, side).start())
 
     @pl.when(s == 0)
     def _():
         fresh.start()
-        for side in range(2):
-            @pl.when(sends_to[side])
-            def _(side=side):
-                fresh_edge(side).start()
 
     for copy in loads[1]:
         copy.start()
@@ -140,28 +168,21 @@
     for h in range(2):
         for at in (0, cols + 1):
             acc[h, :, at] = jnp.zeros((half, height, 3 * channels), f32)
-    for side in range(2):
-        @pl.when(jnp.logical_not(takes_from[side]))
-        def _(side=side):
-            raw_edge[:, side] = jnp.zeros((ticks, frames, cols, 2, channels), bf16)
-            second_edge[:, side] = jnp.zeros((ticks, frames, cols, 2, channels), bf16)
-            fcache_edge[side] = jnp.zeros((2, cols, 2, channels), bf16)
-            scache_edge[side] = jnp.zeros((2, cols, 2, channels), bf16)
 
     def put(window, f, plane, values):
         flat = values.reshape(cols * height, channels).astype(bf16)
         window[f, :, plane * channels : (plane + 1) * channels] = flat
 
-    def put_shifted(window, f, above, below, prepare):
-        values = window[f, :, 0:channels].astype(f32).reshape(cols, height, channels)
-        which = lax.broadcasted_iota(jnp.int32, (cols, 2, channels), 1)
-        pair = prepare(jnp.where(which == 1, above.astype(f32), below.astype(f32)))
-        down, up = with_neighbours(values, pair[:, 1:2], pair[:, 0:1])
-        put(window, f, 1, down)
-        put(window, f, 2, up)
-
-    for copy in local:
-        copy.wait()
+    def put_shifted(window, first, edges, prepare):
+        rows = prepare(edges.astype(f32))
+        for k in range(half):
+            values = window[first + k, :, 0:channels].astype(f32).reshape(cols, height, channels)
+            down, up = with_neighbours(
+                values, rows[:, k : k + 1], rows[:, half + k : half + k + 1]
+            )
+            put(window, first + k, 1, down)
+            put(window, first + k, 2, up)
+
     for window, cache in ((x1, fcache), (x2, scache)):
         for f in range(2):
             put(window, f, 0, cache[f].astype(f32))
@@ -193,10 +214,6 @@
         live = counts[sections - 1 - s + tick]
 
         def first_start(h):
-            @pl.when((tick > 0) & (s == 0) & (h == 0))
-            def _():
-                fresh.wait()
-
             @pl.when((tick > 0) & (s > 0))
             def _():
                 block(h).wait_recv()
@@ -219,40 +236,34 @@
         def first_end(h):
             @pl.when((tick == 0) & (h == 0))
             def _():
-                for side in range(2):
-                    @pl.when(takes_from[side])
-                    def _(side=side):
-                        for copy in start_edges(side):
-                            copy.wait_recv()
-
-                for window, rows in ((x1, fcache_edge), (x2, scache_edge)):
-                    for f in range(2):
-                        put_shifted(window, f, rows[0, f], rows[1, f], lambda pair: pair)
-
+                for kind in range(2):
+                    each_side(takes_from, lambda side: start_edge(kind, side).wait_recv())
+                put_shifted(x1, 0, fcache_edge[...], lambda rows: rows)
+
+            @pl.when((tick == 0) & (h == 1))
+            def _():
+                each_side(takes_from, lambda side: start_edge(2, side).wait_recv())
+
+            for k in range(2):
+                @pl.when((tick > 0) & (s == 0) & (h == k))
+                def _(k=k):
+                    each_side(takes_from, lambda side: start_edge(4 + k, side).wait_recv())
+
+            @pl.when((tick > 0) & (s > 0))
+            def _():
+                each_side(takes_from, lambda side: block_edge(h, side).wait_recv())
+
+            row = lax.broadcasted_iota(jnp.int32, (cols, 2 * half, 1), 1)
+            alive = h * half + row % half < live
+            put_shifted(
+                x1, 2 + h * half, raw_edge[tick, h],
+                lambda rows: normed(jnp.where(alive, rows, 0.0), first_gain[...]),
+            )
+
+            @pl.when((tick == 0) & (h == 0))
+            def _():
                 for copy in loads[1]:
                     copy.wait()
-
-            @pl.when((tick > 0) & (s == 0) & (h == 0))
-            def _():
-                for side in range(2):
-                    @pl.when(takes_from[side])
-                    def _(side=side):
-                        fresh_edge(side).wait_recv()
-
-            @pl.when((tick > 0) & (s > 0))
-            def _():
-                for side in range(2):
-                    @pl.when(takes_from[side])
-                    def _(side=side):
-                        block_edge(h, side).wait_recv()
-
-            @pl.loop(0, half)
-            def _(i):
-                f = h * half + i
-                put_shifted(
-                    x1, 2 + f, raw_edge[tick, 0, f], raw_edge[tick, 1, f],
-                    lambda pair: normed(jnp.where(f < live, pair, 0.0), first_gain[...]),
-                )
 
             acc[h, :, 1 : cols + 1] += part(
                 x1, w1, h, [(a, 1, 3) for a in range(3)], len(first_a)
@@ -262,14 +273,16 @@
             def _(i):
                 f = h * half + i
                 hidden = jnp.where(f < live, summed(h, i, first_bias[...]), 0.0)
-                values = normed(hidden, second_gain[...])
-                second_in[tick, f] = values.astype(bf16)
-                put(x2, 2 + f, 0, values)
-
-            for side in range(2):
-                @pl.when(sends_to[side])
-                def _(side=side):
-                    second_rows(tick, h, side).start()
+                put(x2, 2 + f, 0, normed(hidden, second_gain[...]))
+
+            pack(
+                second_packed.at[tick, h],
+                [
+                    x2[2 + h * half + k, :, 0:channels].astype(f32).reshape(cols, height, channels)
+                    for k in range(half)
+                ],
+            )
+            each_side(sends_to, lambda side: second_rows(tick, h, side).start())
 
         @pl.loop(0, 4)
         def _(slot):
@@ -290,20 +303,23 @@
             def _():
                 for copy in loads[2]:
                     copy.wait()
+                each_side(takes_from, lambda side: start_edge(3, side).wait_recv())
+                put_shifted(x2, 0, scache_edge[...], lambda rows: rows)
+
+            @pl.when((tick == 0) & (h == 0) & (s == 0))
+            def _():
+                fresh.wait()
+                for k in range(2):
+                    pack(
+                        packed.at[4 + k],
+                        [raw[1, k * half + m].astype(f32) for m in range(half)],
+                    )
+                    each_side(sends_to, lambda side: start_edge(4 + k, side).start())
 
             acc[h, :, 1 : cols + 1] = part(x2, w2, h, [(0, 0, 3), (1, 0, 1), (2, 0, 1)], 0)
 
-            for side in range(2):
-                @pl.when(takes_from[side])
-                def _(side=side):
-                    second_rows(tick, h, side).wait_recv()
-
-            @pl.loop(0, half)
-            def _(i):
-                f = h * half + i
-                put_shifted(
-                    x2, 2 + f, second_edge[tick, 0, f], second_edge[tick, 1, f], lambda pair: pair
-                )
+            each_side(takes_from, lambda side: second_rows(tick, h, side).wait_recv())
+            put_shifted(x2, 2 + h * half, second_edge[tick, h], lambda rows: rows)
 
             @pl.when((tick == 0) & (h == 0))
             def _():
@@ -321,10 +337,11 @@
             @pl.when((tick == 0) & (s < sections - 1))
             def _():
                 block(h).start()
-                for side in range(2):
-                    @pl.when(sends_to[side])
-                    def _(side=side):
-                        block_edge(h, side).start()
+                pack(
+                    packed.at[6 + h],
+                    [out[0, 0, h * half + k].astype(f32) for k in range(half)],
+                )
+                each_side(sends_to, lambda side: block_edge(h, side).start())
 
         for window in (x1, x2):
             for j in range(2):
@@ -335,25 +352,26 @@
             values = window[j, :, 0:channels].astype(f32)
             target[0, j] = values.reshape(cols, height, channels).astype(bf16)
 
-    for side in range(2):
-        @pl.when(sends_to[side])
-        def _(side=side):
-            for copy in start_edges(side):
-                copy.wait_send()
-
-            @pl.loop(0, ticks)
-            def _(tick):
-                for h in range(2):
-                    second_rows(tick, h, side).wait_send()
-
-            @pl.when(s == 0)
-            def _():
-                fresh_edge(side).wait_send()
-
-            @pl.when(s < sections - 1)
-            def _():
-                for h in range(2):
-                    block_edge(h, side).wait_send()
+    def sent(side):
+        for kind in range(4):
+            start_edge(kind, side).wait_send()
+
+        @pl.loop(0, ticks)
+        def _(tick):
+            for h in range(2):
+                second_rows(tick, h, side).wait_send()
+
+        @pl.when(s == 0)
+        def _():
+            for kind in range(4, 6):
+                start_edge(kind, side).wait_send()
+
+        @pl.when(s < sections - 1)
+        def _():
+            for h in range(2):
+                block_edge(h, side).wait_send()
+
+    each_side(sends_to, sent)
 
     @pl.when(s < sections - 1)
     def _():
@@ -393,7 +411,7 @@
         jax.ShapeDtypeStruct(first_cache.shape, bf16),
         jax.ShapeDtypeStruct(second_cache.shape, bf16),
     )
-    transfers = 14 + 4 * ticks
+    transfers = 18 + 4 * ticks
     results = pl.pallas_call(
         kernel,
         out_shape=tuple(pltpu.VMEM(v.shape, v.dtype) for v in shapes),
@@ -402,13 +420,14 @@
         out_specs=(inside, inside, inside),
         scratch_shapes=[
             pltpu.VMEM((ticks, frames, cols, height, channels), bf16),
-            pltpu.VMEM((ticks, 2, frames, cols, 2, channels), bf16),
+            pltpu.VMEM((ticks, 2, cols, frames, channels), bf16),
             pltpu.VMEM((2, cols, height, channels), bf16),
-            pltpu.VMEM((2, 2, cols, 2, channels), bf16),
+            pltpu.VMEM((cols, 4, channels), bf16),
             pltpu.VMEM((2, cols, height, channels), bf16),
-            pltpu.VMEM((2, 2, cols, 2, channels), bf16),
-            pltpu.VMEM((ticks, frames, cols, height, channels), bf16),
-            pltpu.VMEM((ticks, 2, frames, cols, 2, channels), bf16),
+            pltpu.VMEM((cols, 4, channels), bf16),
+            pltpu.VMEM((ticks, 2, cols, frames, channels), bf16),
+            pltpu.VMEM((8, 2, cols, frames // 2, channels), bf16),
+            pltpu.VMEM((ticks, 2, 2, cols, frames // 2, channels), bf16),
             pltpu.VMEM((frames + 2, cols * height, 3 * channels), bf16),
             pltpu.VMEM((frames + 2, cols * height, 3 * channels), bf16),
             pltpu.VMEM((9 * channels, 3 * channels), bf16),

time: 36.5 us -> 31.2 us (0.85)
  Pallas kernels: 35.7 us -> 30.4 us
    pallas_call x1, Pallas kernels: 34.7 us -> 29.5 us  [on_device(): pl.pallas_call(kernel, out_shape=tuple((pltpu.VMEM(v.shape, v.dtype) for...]
where the time goes in v3:
time: 31.2 us; the launch traced here: 31 us
  Pallas kernels  30.4 us (97%)
  between operations  0.64 us (2%)
    pallas_call x1, Pallas kernels, on_device(): pl.pallas_call(kernel, out_shape=tuple((pltpu.VMEM(v.shape, v.dtype) for...  29.5 us
    pallas_call x1, Pallas kernels, on_device(): pl.pallas_call(deliver, out_shape=shapes, in_specs=[inside] * 3, out_spec...  0.93 us

profile of v3, /device:TPU:0, one launch (start us, length us, event | category | flops | bytes accessed | tf_op | source)
XLA Modules:
  0.0 31.0 jit_solution(1273430376192813680)
XLA Ops:
  0.6 29.5 %shard_map.130 = (bf16[2,1,4,12,8,384]{5,4,3,2,1,0:T(8,128)(2,1)S(1)}, bf16[1,2,12,8,384]{4,3,2,1,0:T(8,128)(2,1)S(1)}, bf16[1,2,12,8,384]{4,3,2,1,0:T(8,128)(2,1)S(1)}) custom-call(s32[5]{0:T(128)} %counts.1, bf16[1,4,12,8,384]{4,3,2,1,0:T(8,128)(2,1)} %bitcast.7, bf16[1,4,12,8,384]{4,3,2,1,0:T(8,128)(2,1)} %bitcast.8, bf16[1,2,12,8,384]{4,3,2,1,0:T(8,128)(2,1)} %bitcast.9, ...), custom_call_target="tpu_custom_call" | custom-call | tf_op jit(solution)/shard_map/pallas_call | solution.py:415
  30.1 0.9 %shard_map.131 = (bf16[2,1,4,12,8,384]{5,4,3,2,1,0:T(8,128)(2,1)}, bf16[1,2,12,8,384]{4,3,2,1,0:T(8,128)(2,1)}, bf16[1,2,12,8,384]{4,3,2,1,0:T(8,128)(2,1)}) custom-call(bf16[2,1,4,12,8,384]{5,4,3,2,1,0:T(8,128)(2,1)S(1)} %get-tuple-element.9.refs_0_, bf16[1,2,12,8,384]{4,3,2,1,0:T(8,128)(2,1)S(1)} %get-tuple-element.10.refs_1_, ...), custom_call_target="tpu_custom_call" | custom-call | tf_op jit(solution)/shard_map/pallas_call | solution.py:448

commit v4 on v3

--- a/solution.py
+++ b/solution.py
@@ -77,7 +77,7 @@
         def _(i=i, j=j):
             pl.semaphore_signal(barrier, inc=1, device_id=(s + i, p + j), device_id_type=MESH)
 
-    for copy in loads[0]:
+    for copy in loads[0] + loads[1]:
         copy.start()
 
     def remote(source, target, k, i, j):
@@ -161,9 +161,6 @@
     @pl.when(s == 0)
     def _():
         fresh.start()
-
-    for copy in loads[1]:
-        copy.start()
 
     for h in range(2):
         for at in (0, cols + 1):
@@ -214,16 +211,6 @@
         live = counts[sections - 1 - s + tick]
 
         def first_start(h):
-            @pl.when((tick > 0) & (s > 0))
-            def _():
-                block(h).wait_recv()
-
-            @pl.loop(0, half)
-            def _(i):
-                f = h * half + i
-                values = jnp.where(f < live, raw[tick, f].astype(f32), 0.0)
-                put(x1, 2 + f, 0, normed(values, first_gain[...]))
-
             @pl.when((tick == 0) & (h == 0))
             def _():
                 for copy in loads[0]:
@@ -231,6 +218,15 @@
                 for copy in loads[2] + loads[3]:
                     copy.start()
 
+            @pl.when((tick > 0) & (s > 0))
+            def _():
+                block(h).wait_recv()
+
+            for i in range(half):
+                f = h * half + i
+                values = jnp.where(f < live, raw[tick, f].astype(f32), 0.0)
+                put(x1, 2 + f, 0, normed(values, first_gain[...]))
+
             acc[h, :, 1 : cols + 1] = part(x1, w1, h, [(a, 0, 1) for a in range(3)], 0)
 
         def first_end(h):
@@ -239,6 +235,8 @@
                 for kind in range(2):
                     each_side(takes_from, lambda side: start_edge(kind, side).wait_recv())
                 put_shifted(x1, 0, fcache_edge[...], lambda rows: rows)
+                for copy in loads[1]:
+                    copy.wait()
 
             @pl.when((tick == 0) & (h == 1))
             def _():
@@ -260,17 +258,11 @@
                 lambda rows: normed(jnp.where(alive, rows, 0.0), first_gain[...]),
             )
 
-            @pl.when((tick == 0) & (h == 0))
-            def _():
-                for copy in loads[1]:
-                    copy.wait()
-
             acc[h, :, 1 : cols + 1] += part(
                 x1, w1, h, [(a, 1, 3) for a in range(3)], len(first_a)
             )
 
-            @pl.loop(0, half)
-            def _(i):
+            for i in range(half):
                 f = h * half + i
                 hidden = jnp.where(f < live, summed(h, i, first_bias[...]), 0.0)
                 put(x2, 2 + f, 0, normed(hidden, second_gain[...]))
@@ -301,7 +293,7 @@
         def _(h):
             @pl.when((tick == 0) & (h == 0))
             def _():
-                for copy in loads[2]:
+                for copy in loads[2] + loads[3]:
                     copy.wait()
                 each_side(takes_from, lambda side: start_edge(3, side).wait_recv())
                 put_shifted(x2, 0, scache_edge[...], lambda rows: rows)
@@ -321,15 +313,9 @@
             each_side(takes_from, lambda side: second_rows(tick, h, side).wait_recv())
             put_shifted(x2, 2 + h * half, second_edge[tick, h], lambda rows: rows)
 
-            @pl.when((tick == 0) & (h == 0))
-            def _():
-                for copy in loads[3]:
-                    copy.wait()
-
             acc[h, :, 1 : cols + 1] += part(x2, w2, h, [(1, 1, 3), (2, 1, 3)], len(second_a))
 
-            @pl.loop(0, half)
-            def _(i):
+            for i in range(half):
                 f = h * half + i
                 total = summed(h, i, second_bias[...]) + raw[tick, f].astype(f32)
                 out[tick, 0, f] = jnp.where(f < live, total, 0.0).astype(bf16)

time: 31.2 us -> 29.3 us (0.939)
  Pallas kernels: 30.4 us -> 28.5 us
    pallas_call x1, Pallas kernels: 29.5 us -> 27.6 us  [on_device(): pl.pallas_call(kernel, out_shape=tuple((pltpu.VMEM(v.shape, v.dtype) for...]
where the time goes in v4:
time: 29.3 us; the launch traced here: 29.2 us
  Pallas kernels  28.5 us (97%)
  between operations  0.64 us (2%)
    pallas_call x1, Pallas kernels, on_device(): pl.pallas_call(kernel, out_shape=tuple((pltpu.VMEM(v.shape, v.dtype) for...  27.6 us
    pallas_call x1, Pallas kernels, on_device(): pl.pallas_call(deliver, out_shape=shapes, in_specs=[inside] * 3, out_spec...  0.93 us

profile of v4, /device:TPU:0, one launch (start us, length us, event | category | flops | bytes accessed | tf_op | source)
XLA Modules:
  0.0 29.2 jit_solution(4808910193913843522)
XLA Ops:
  0.6 27.6 %shard_map.130 = (bf16[2,1,4,12,8,384]{5,4,3,2,1,0:T(8,128)(2,1)S(1)}, bf16[1,2,12,8,384]{4,3,2,1,0:T(8,128)(2,1)S(1)}, bf16[1,2,12,8,384]{4,3,2,1,0:T(8,128)(2,1)S(1)}) custom-call(s32[5]{0:T(128)} %counts.1, bf16[1,4,12,8,384]{4,3,2,1,0:T(8,128)(2,1)} %bitcast.7, bf16[1,4,12,8,384]{4,3,2,1,0:T(8,128)(2,1)} %bitcast.8, bf16[1,2,12,8,384]{4,3,2,1,0:T(8,128)(2,1)} %bitcast.9, ...), custom_call_target="tpu_custom_call" | custom-call | tf_op jit(solution)/shard_map/pallas_call | solution.py:401
  28.3 0.9 %shard_map.131 = (bf16[2,1,4,12,8,384]{5,4,3,2,1,0:T(8,128)(2,1)}, bf16[1,2,12,8,384]{4,3,2,1,0:T(8,128)(2,1)}, bf16[1,2,12,8,384]{4,3,2,1,0:T(8,128)(2,1)}) custom-call(bf16[2,1,4,12,8,384]{5,4,3,2,1,0:T(8,128)(2,1)S(1)} %get-tuple-element.9.refs_0_, bf16[1,2,12,8,384]{4,3,2,1,0:T(8,128)(2,1)S(1)} %get-tuple-element.10.refs_1_, ...), custom_call_target="tpu_custom_call" | custom-call | tf_op jit(solution)/shard_map/pallas_call | solution.py:434

commit v5 on v4

--- a/solution.py
+++ b/solution.py
@@ -24,8 +24,9 @@
 
 
 def kernel(
-    counts, held, incoming, first_cache, second_cache, first_kernel, first_bias, first_gain,
-    second_kernel, second_bias, second_gain, out, first_out, second_out,
+    counts_in, held, incoming, first_cache, second_cache, first_kernel, first_bias_in,
+    first_gain_in, second_kernel, second_bias_in, second_gain_in, out, first_out, second_out,
+    counts, first_bias, first_gain, second_bias, second_gain,
     raw, raw_edge, fcache, fcache_edge, scache, scache_edge, second_edge, packed, second_packed,
     x1, x2, w1, w2, acc, local_sem, w_sem, send_sem, recv_sem,
 ):
@@ -40,6 +41,14 @@
         pltpu.make_async_copy(held.at[0], raw.at[0], local_sem.at[0]),
         pltpu.make_async_copy(first_cache.at[0], fcache, local_sem.at[1]),
         pltpu.make_async_copy(second_cache.at[0], scache, local_sem.at[2]),
+    ]
+    small = [
+        (counts_in, counts), (first_bias_in, first_bias), (first_gain_in, first_gain),
+        (second_bias_in, second_bias), (second_gain_in, second_gain),
+    ]
+    local += [
+        pltpu.make_async_copy(source, target, local_sem.at[4 + k])
+        for k, (source, target) in enumerate(small)
     ]
     for copy in local:
         copy.start()
@@ -401,10 +410,11 @@
     results = pl.pallas_call(
         kernel,
         out_shape=tuple(pltpu.VMEM(v.shape, v.dtype) for v in shapes),
-        in_specs=[pl.BlockSpec(memory_space=pltpu.SMEM)] + [anywhere] * 5
-        + [inside, inside, anywhere, inside, inside],
+        in_specs=[anywhere] * 11,
         out_specs=(inside, inside, inside),
         scratch_shapes=[
+            pltpu.SMEM(frame_counts.shape, frame_counts.dtype),
+            *(pltpu.VMEM((1, channels), jnp.float32) for _ in range(4)),
             pltpu.VMEM((ticks, frames, cols, height, channels), bf16),
             pltpu.VMEM((ticks, 2, cols, frames, channels), bf16),
             pltpu.VMEM((2, cols, height, channels), bf16),
@@ -419,7 +429,7 @@
             pltpu.VMEM((9 * channels, 3 * channels), bf16),
             pltpu.VMEM((9 * channels, 3 * channels), bf16),
             pltpu.VMEM((2, frames // 2, cols + 2, height, 3 * channels), jnp.float32),
-            pltpu.SemaphoreType.DMA((4,)),
+            pltpu.SemaphoreType.DMA((9,)),
             pltpu.SemaphoreType.DMA((4,)),
             pltpu.SemaphoreType.DMA((transfers,)),
             pltpu.SemaphoreType.DMA((transfers,)),

time: 29.3 us -> 28.4 us (0.969)
  Pallas kernels: 28.5 us -> 27.6 us
    pallas_call x1, Pallas kernels: 27.6 us -> 26.7 us  [on_device(): pl.pallas_call(kernel, out_shape=tuple((pltpu.VMEM(v.shape, v.dtype) for...]
where the time goes in v5:
time: 28.4 us; the launch traced here: 28.3 us
  Pallas kernels  27.6 us (97%)
  between operations  0.64 us (2%)
    pallas_call x1, Pallas kernels, on_device(): pl.pallas_call(kernel, out_shape=tuple((pltpu.VMEM(v.shape, v.dtype) for...  26.7 us
    pallas_call x1, Pallas kernels, on_device(): pl.pallas_call(deliver, out_shape=shapes, in_specs=[inside] * 3, out_spec...  0.93 us

profile of v5, /device:TPU:0, one launch (start us, length us, event | category | flops | bytes accessed | tf_op | source)
XLA Modules:
  0.0 28.3 jit_solution(15759653496200424227)
XLA Ops:
  0.6 26.7 %shard_map.130 = (bf16[2,1,4,12,8,384]{5,4,3,2,1,0:T(8,128)(2,1)S(1)}, bf16[1,2,12,8,384]{4,3,2,1,0:T(8,128)(2,1)S(1)}, bf16[1,2,12,8,384]{4,3,2,1,0:T(8,128)(2,1)S(1)}) custom-call(s32[5]{0:T(128)} %counts_in.1, bf16[1,4,12,8,384]{4,3,2,1,0:T(8,128)(2,1)} %bitcast.7, bf16[1,4,12,8,384]{4,3,2,1,0:T(8,128)(2,1)} %bitcast.8, ...), custom_call_target="tpu_custom_call" | custom-call | tf_op jit(solution)/shard_map/pallas_call | solution.py:410
  27.3 0.9 %shard_map.131 = (bf16[2,1,4,12,8,384]{5,4,3,2,1,0:T(8,128)(2,1)}, bf16[1,2,12,8,384]{4,3,2,1,0:T(8,128)(2,1)}, bf16[1,2,12,8,384]{4,3,2,1,0:T(8,128)(2,1)}) custom-call(bf16[2,1,4,12,8,384]{5,4,3,2,1,0:T(8,128)(2,1)S(1)} %get-tuple-element.9.refs_0_, bf16[1,2,12,8,384]{4,3,2,1,0:T(8,128)(2,1)S(1)} %get-tuple-element.10.refs_1_, ...), custom_call_target="tpu_custom_call" | custom-call | tf_op jit(solution)/shard_map/pallas_call | solution.py:444
